TPU v7x, 512 devices: a whole 4x8x8 slice. The times are simulated.
512 devices in a mesh: seq: 64 (over z_hi, y, core), head: 8 (over x, z_lo).
Axes of the slice: x: 4, y: 8, z: 8 (z_hi: 4, z_lo: 2; z = z_hi * 2 + z_lo), core: 2. Of those that a mesh axis runs over, the one named last changes fastest.
Arguments:
- tokens: bfloat16 [8192, 2880], P('seq'), may hold values from -80 to 80
- gain: float32 [2880], replicated, may hold values from 0.1 to 1.9
- w_query: bfloat16 [2880, 4096], P('seq', 'head'), may hold values from -4 to 4
- w_key: bfloat16 [2880, 512], P('seq', 'head'), may hold values from -1 to 1
- w_value: bfloat16 [2880, 512], P('seq', 'head'), may hold values from -0.109375 to 0.109375
- w_out: bfloat16 [2880, 4096], P('seq', 'head'), may hold values from -0.09375 to 0.09375
- w_gate: float32 [2880], replicated, may hold values from -0.109375 to 0.109375
- steering: bfloat16 [16, 2880], replicated, may hold values from -5 to 5
- segment_ids: int32 [8192], P('seq'), may hold values from 0 to 31, never falling along the last dimension, each value on 1 to 512 neighbouring positions
- steer_index: int32 [8192], P('seq'), may hold values from 0 to 15
- grad_out: bfloat16 [8192, 2880], P('seq'), may hold values from -6 to 6
Outputs:
- layer_out: bfloat16 [8192, 2880], P('seq', 'head')
- grad_tokens: bfloat16 [8192, 2880], P('seq', 'head')
- steer_grad: float32 [16, 2880], P(None, 'head')
Inputs may be any that keep to these rules, and one draw needn't show every extreme that they name: `segment_ids`: the ids never fall along the tokens; each id names one packed document of at most 512 tokens.
All inputs are finite; a program needn't handle non-finite values.
Results may differ from a plain program's by a relative error of at most 0.011.
Values may be sent and summed in bfloat16 or wider, within the bound.
No kernel may reach another device: no remote copies, remote signals or barrier semaphores. Data moves between devices by JAX's collectives and lax.ppermute only.
A program may use at most 64 MiB of HBM per device.

v0:
```python
import jax
import jax.numpy as jnp
from jax import lax
from jax.sharding import Mesh, PartitionSpec as P

HD = 64
WIN = 128
EPSILON = 1e-05
HIGHEST = lax.Precision.HIGHEST
SEQ = ("zh", "y", "core")
HEAD = ("x", "zl")
F32 = jnp.float32
BF16 = jnp.bfloat16
PAD = 48


def shifted(value, by):
    count = lax.axis_size(SEQ)
    pairs = [(i, i + by) for i in range(count) if 0 <= i + by < count]
    return lax.ppermute(value, SEQ, pairs)


def gathered(value, axes):
    count = lax.axis_size(axes)
    spread = jnp.broadcast_to(value[None], (count,) + value.shape)
    return lax.all_to_all(spread, axes, 0, 0)


def dot(left, right, dims, **kw):
    return lax.dot_general(left, right, (dims, ((), ())), preferred_element_type=F32, **kw)


def blocked(rows):
    width = rows.shape[-1]
    parts = rows.reshape(4, 8, 2, -1, width).transpose(1, 0, 2, 3, 4)
    parts = jnp.pad(parts, ((0, 0), (0, 0), (0, 0), (0, PAD - parts.shape[3]), (0, 0)))
    return parts.reshape(-1, width)


def for_heads(rows):
    width = rows.shape[-1]
    parts = rows.reshape(2, 4, 4, 2, PAD, width).transpose(2, 0, 1, 3, 4, 5)
    return parts.reshape(8, -1, width)


def unpadded(rows, row_count):
    width = rows.shape[-1]
    return rows.reshape(8, PAD, width)[:, : row_count // 8].reshape(row_count, width)


def split3(value):
    high = lax.reduce_precision(value, 8, 7)
    rest = value - high
    mid = lax.reduce_precision(rest, 8, 7)
    low = lax.reduce_precision(rest - mid, 8, 7)
    return jnp.stack([high, mid, low])


def shards(
    tokens,
    gain,
    w_query,
    w_key,
    w_value,
    w_out,
    w_gate,
    steering,
    segment_ids,
    steer_index,
    grad_out,
):
    row_count, model_width = tokens.shape
    share = model_width // 8
    start = lax.axis_index(HEAD) * share
    padded = lambda w: jnp.pad(w, ((0, PAD - w.shape[0]), (0, 0)))
    both = jnp.stack([padded(w_query), padded(w_out)])
    half = both.shape[2] // 2
    both = both.reshape(2, PAD, 2, half).transpose(2, 0, 1, 3)
    sent = jnp.broadcast_to(both[None], (4,) + both.shape).reshape((8,) + both.shape[1:])
    near = lax.all_to_all(sent, ("zh", "core"), 0, 0)
    q_own = lax.all_gather(near[:, 0], "y", axis=0, tiled=True).reshape(-1, half)
    o_own = lax.all_gather(near[:, 1], "y", axis=0, tiled=True).reshape(-1, half)
    w_kv = padded(jnp.concatenate([w_key, w_value], axis=1))
    kv_near = lax.all_gather(w_kv, ("zh",), axis=0, tiled=False)
    kv_all = lax.all_gather(kv_near, ("y", "core"), axis=0, tiled=False)
    kv_all = kv_all.reshape(8, 2, 4, PAD, 2 * HD).transpose(0, 2, 1, 3, 4).reshape(-1, 2 * HD)
    flip = [(0, 1), (1, 0)]
    q_oth = lax.ppermute(q_own, "core", flip)
    o_oth = lax.ppermute(o_own, "core", flip)
    tok = tokens.T.astype(F32)
    inverse = lax.rsqrt(jnp.mean(tok * tok, axis=0, keepdims=True) + EPSILON)
    unit = tok * inverse
    normed = (unit * gain[:, None]).astype(BF16)
    normed_b = blocked(normed)
    unit_b = blocked(unit * gain[:, None])
    grad_t = grad_out.T
    grad_b = blocked(grad_t)
    gate = jax.nn.sigmoid(jnp.sum(normed.astype(F32) * w_gate[:, None], axis=0))
    one_hot = steer_index[None, :] == lax.broadcasted_iota(jnp.int32, (16, row_count), 0)
    products = dot(steering, grad_t, ((1,), (0,)))
    grad_logit = gate * (1.0 - gate) * jnp.sum(jnp.where(one_hot, products, 0.0), axis=0)
    steer_share = lax.dynamic_slice_in_dim(steering, start, share, 1)
    steer_rows = dot(steer_share, one_hot.astype(BF16), ((0,), (0,)))
    grad_share = lax.dynamic_slice_in_dim(grad_t, start, share, 0).astype(F32)
    steer_part = dot(
        one_hot.astype(F32), gate[None, :] * grad_share, ((1,), (1,)), precision=HIGHEST
    )
    steer_near = jnp.sum(gathered(steer_part, ("zh", "core")), axis=0)
    steer_grad = jnp.sum(gathered(steer_near, ("y",)), axis=0)
    halo_seg = shifted(segment_ids, 1)
    halo_seg = jnp.where(lax.axis_index(SEQ) > 0, halo_seg, -1)
    kv = dot(kv_all, normed_b, ((0,), (0,))).astype(BF16)
    kv_halo = shifted(kv, 1)
    wide = jnp.concatenate([kv_halo, kv], axis=1)
    keys, values = (wide[:HD], wide[HD:])
    wide_seg = jnp.concatenate([halo_seg, segment_ids])
    query_pos = lax.broadcasted_iota(jnp.int32, (row_count, 2 * row_count), 0)
    key_pos = lax.broadcasted_iota(jnp.int32, (row_count, 2 * row_count), 1) - WIN
    distance = query_pos - key_pos
    mask = (distance >= 0) & (distance < WIN) & (segment_ids[:, None] == wide_seg[None, :])
    query = jnp.concatenate(
        [
            dot(q_own, normed_b, ((0,), (0,))).astype(BF16),
            dot(q_oth, normed_b, ((0,), (0,))).astype(BF16),
        ]
    ).reshape(8, HD, row_count)
    scores = jnp.einsum("hdq,dk->hqk", query, keys, preferred_element_type=F32) * HD ** (-0.5)
    scores = jnp.where(mask[None], scores, -jnp.inf)
    raised = jnp.exp(scores - jnp.max(scores, axis=-1, keepdims=True))
    probs = raised / jnp.sum(raised, axis=-1, keepdims=True)
    probs_b = probs.astype(BF16)
    mixed = jnp.einsum("hqk,dk->hdq", probs_b, values, preferred_element_type=F32)
    mixed = mixed.astype(BF16).reshape(2, half, row_count)
    term = dot(o_own, mixed[0], ((1,), (0,))) + dot(o_oth, mixed[1], ((1,), (0,)))
    attn = lax.all_to_all(for_heads(term.astype(BF16)), HEAD, 0, 0)
    attn_share = unpadded(jnp.sum(attn.astype(F32), axis=0), share)
    token_share = lax.dynamic_slice_in_dim(tokens.T, start, share, 0).astype(F32)
    layer_out = (token_share + attn_share + gate[None, :] * steer_rows).astype(BF16)
    grad_mixed = jnp.concatenate(
        [
            dot(o_own, grad_b, ((0,), (0,))).astype(BF16),
            dot(o_oth, grad_b, ((0,), (0,))).astype(BF16),
        ]
    ).reshape(8, HD, row_count)
    grad_values = jnp.einsum("hqk,hdq->dk", probs_b, grad_mixed, preferred_element_type=F32)
    grad_prob = jnp.einsum("hdq,dk->hqk", grad_mixed, values, preferred_element_type=F32)
    delta = jnp.sum(probs * grad_prob, axis=-1, keepdims=True)
    grad_scores = (probs * (grad_prob - delta) * HD ** (-0.5)).astype(BF16)
    grad_query = jnp.einsum("hqk,dk->hdq", grad_scores, keys, preferred_element_type=F32)
    grad_query = grad_query.astype(BF16).reshape(2, half, row_count)
    grad_keys = jnp.einsum("hqk,hdq->dk", grad_scores, query, preferred_element_type=F32)
    grad_kv = jnp.concatenate([grad_keys, grad_values])
    returned = shifted(grad_kv[:, :WIN].astype(BF16), -1)
    grad_kv = (grad_kv[:, WIN:] + returned.astype(F32)).astype(BF16)
    terms = (
        dot(q_own, grad_query[0], ((1,), (0,)))
        + dot(q_oth, grad_query[1], ((1,), (0,)))
        + dot(kv_all, grad_kv, ((1,), (0,)))
    ).astype(BF16)
    row_part = split3(jnp.sum(terms.astype(F32) * unit_b, axis=0)).astype(BF16)
    extra = jnp.broadcast_to(jnp.pad(row_part, ((0, 13), (0, 0)))[None], (8, 16, row_count))
    back = lax.all_to_all(jnp.concatenate([for_heads(terms), extra], axis=1), HEAD, 0, 0)
    back = jnp.sum(back.astype(F32), axis=0)
    gain_share = lax.dynamic_slice_in_dim(gain, start, share, 0)[:, None]
    gate_share = lax.dynamic_slice_in_dim(w_gate, start, share, 0)[:, None]
    total = unpadded(back[: 8 * PAD], share) + grad_logit[None, :] * gate_share
    gate_total = jnp.sum(unit * (gain * w_gate)[:, None], axis=0)
    row_total = jnp.sum(back[8 * PAD : 8 * PAD + 3], axis=0) + grad_logit * gate_total
    unit_share = token_share * inverse
    scaled = total * gain_share
    grad_tokens = (
        grad_share + inverse * (scaled - unit_share * (row_total / model_width)[None, :])
    ).astype(BF16)
    return (layer_out.T, grad_tokens.T, steer_grad)


def solution(mesh):
    split = Mesh(mesh.devices.reshape(4, 8, 2, 4, 2), SEQ + HEAD)
    placed = (
        P(SEQ, None),
        P(),
        P(SEQ, HEAD),
        P(SEQ, HEAD),
        P(SEQ, HEAD),
        P(SEQ, HEAD),
        P(),
        P(),
        P(SEQ),
        P(SEQ),
        P(SEQ, None),
    )
    return jax.shard_map(
        shards,
        mesh=split,
        in_specs=placed,
        out_specs=(P(SEQ, HEAD), P(SEQ, HEAD), P(None, HEAD)),
        check_vma=False,
    )
```

profile of v0, /device:TPU:2, one launch (start us, length us, event | category | flops | bytes accessed | tf_op | source)
XLA Modules:
  0.0 241.0 jit_solution(13641125180174731504)
XLA Ops:
  9.2 25.7 %all_to_all.25 = bf16[8,2,48,256]{3,2,1,0:T(8,128)(2,1)S(1)} all-to-all(bf16[8,2,48,256]{3,2,1,0:T(8,128)(2,1)S(1)} %bitcast.165), channel_id=1, replica_groups=mesh['zh'=4,'y'=8,'core'=2,'x'=4,'zl'=2] {'zh','core'}, dimensions={0} | all-to-all | bytes 786432 | tf_op jit(solution)/shard_map/all_to_all | solution.py:80
  41.1 13.8 %all-gather.1 = bf16[192,128]{1,0:T(8,128)(2,1)S(1)} all-gather(bf16[48,128]{1,0:T(8,128)(2,1)S(1)} %fusion.63), channel_id=3, replica_groups=mesh['zh'=4,'y'=8,'core'=2,'x'=4,'zl'=2] {'zh'}, dimensions={0}, use_global_device_ids=true | all-gather | bytes 61440 | tf_op jit(solution)/shard_map/all_gather | solution.py:84
  54.8 22.2 %all-gather.2 = bf16[64,48,128]{2,1,0:T(8,128)(2,1)S(1)} all-gather(bf16[4,48,128]{2,1,0:T(8,128)(2,1)S(1)} %bitcast.174), channel_id=4, replica_groups=mesh['zh'=4,'y'=8,'core'=2,'x'=4,'zl'=2] {'y','core'}, dimensions={0}, use_global_device_ids=true | all-gather | bytes 835584 | tf_op jit(solution)/shard_map/all_gather | solution.py:85
  77.1 2.2 collective-permute-start.3
  79.8 2.1 collective-permute-start
  81.8 3.2 %fusion.10 = (f32[128]{0:T(128)}, f32[2880,128]{1,0:T(8,128)}) fusion(bf16[128,2880]{0,1:T(8,128)(2,1)S(1)} %copy-done.1, f32[2880]{0:T(1024)S(1)} %mul.187, f32[128]{0:T(128)S(1)} %add_rsqrt_fusion, f32[2880]{0:T(1024)S(1)} %copy-done.13), kind=kLoop, calls=%fused_computation.17 | loop fusion | flops 1843072 | bytes 2235904 | tf_op jit(solution)/shard_map/reduce_sum | solution.py:167
  85.1 33.8 %all-gather.9.cloned.1.call-done = bf16[64,1,48,256]{3,2,1,0:T(8,128)(2,1)} async-done(((bf16[8,1,48,256]{3,2,1,0:T(8,128)(2,1)}), bf16[64,1,48,256]{3,2,1,0:T(8,128)(2,1)}) %all-gather.9.cloned.1.call-update) | async-done | bytes 1572880 | tf_op jit(solution)/shard_map/all_gather | solution.py:81
  118.8 2.0 collective-permute-start.2
  122.5 2.5 %reshape.221 = f32[4,8,2,45,128]{4,3,2,1,0:T(8,128)} reshape(f32[2880,128]{1,0:T(8,128)} %get-tuple-element.9) | data formatting | bytes 2949120 | tf_op jit(solution)/shard_map/reshape | solution.py:35
  125.0 2.8 %copy.63 = f32[8,4,2,45,128]{4,3,2,1,0:T(8,128)} copy(f32[8,4,2,45,128]{4,3,2,0,1:T(8,128)} %bitcast.154) | data formatting | bytes 2949120
  127.8 2.8 %pad.31.clone = f32[8,4,2,48,128]{4,3,2,1,0:T(8,128)} pad(f32[8,4,2,45,128]{4,3,2,1,0:T(8,128)} %copy.63, f32[]{:T(128)} %constant.42.clone.1), padding=0_0x0_0x0_0x0_3x0_0 | pad | bytes 3047428 | tf_op jit(solution)/shard_map/jit(_pad)/pad | solution.py:36
  138.8 7.2 %convolution_bitcast_fusion.2 = f32[64,256]{1,0:T(8,128)S(1)} fusion(bf16[8,64,128]{2,1,0:T(8,128)(2,1)S(1)} %bitcast.176, f32[8,128,256]{2,1,0:T(8,128)S(1)} %fusion.65, f32[8,128,256]{2,1,0:T(8,128)} %get-tuple-element.20, f32[8,128]{1,0:T(8,128)S(1)} %get-tuple-element.19), kind=kOutput, calls=%fused_computation.41 | convolution fusion | flops 35390720 | bytes 2297856 | tf_op jit(solution)/shard_map/hqk,hdq->dk/dot_general | solution.py:151
  146.0 7.3 %fusion.21 = bf16[8,64,128]{2,1,0:T(8,128)(2,1)S(1)} fusion(f32[8,128,256]{2,1,0:T(8,128)S(1)} %fusion.65, bf16[128,128]{0,1:T(8,128)(2,1)S(1)} %fusion.23, bf16[128,128]{0,1:T(8,128)(2,1)S(1)} %collective-permute-done, f32[8,128,256]{2,1,0:T(8,128)} %get-tuple-element.20, f32[8,128]{1,0:T(8,128)S(1)} %get-tuple-element.19), kind=kOutput, calls=%fused_computation.33 | convolution fusion | flops 35521792 | bytes 2297856 | tf_op jit(solution)/shard_map/hqk,dk->hdq/dot_general | solution.py:149
  153.3 3.0 %convolution_bitcast_fusion.1 = f32[64,256]{1,0:T(8,128)S(1)} fusion(bf16[8,64,128]{2,1,0:T(8,128)(2,1)S(1)} %bitcast.169, f32[8,128]{1,0:T(8,128)} %copy-done.25, bf16[8,64,128]{2,1,0:T(8,128)(2,1)} %bitcast.177, pred[128,256]{1,0:T(8,128)(4,1)} %copy-done.19, bf16[128,128]{0,1:T(8,128)(2,1)} %copy-done.15, bf16[128,128]{0,1:T(8,128)(2,1)} %copy-done.17), kind=kOutput, calls=%fused_computation.40 | convolution fusion | flops 68486400 | bytes 430080 | tf_op jit(solution)/shard_map/hqk,hdq->dk/dot_general | solution.py:145
  159.9 2.3 fusion.7
  163.3 5.9 %all-to-all-start.2 = ((bf16[8,400,128]{2,1,0:T(8,128)(2,1)}), bf16[8,400,128]{2,1,0:T(8,128)(2,1)}, u32[]{:S(2)}, u32[]{:S(2)}) async-start(bf16[8,400,128]{2,1,0:T(8,128)(2,1)} %pad_maximum_fusion), calls=%async_computation.2 | async-start | bytes 1638400 | tf_op jit(solution)/shard_map/all_to_all | solution.py:162
  169.2 3.0 %fusion.20 = bf16[8,64,128]{2,1,0:T(8,128)(2,1)S(1)} fusion(bf16[128,128]{0,1:T(8,128)(2,1)S(1)} %copy-done.16, bf16[128,128]{0,1:T(8,128)(2,1)S(1)} %copy-done.18, f32[8,128]{1,0:T(8,128)S(1)} %copy-done.26, bf16[8,64,128]{2,1,0:T(8,128)(2,1)S(1)} %bitcast.178, pred[128,256]{1,0:T(8,128)(4,1)} %copy-done.19), kind=kOutput, calls=%fused_computation.32 | convolution fusion | flops 68617472 | bytes 430080 | tf_op jit(solution)/shard_map/hqk,dk->hdq/dot_general | solution.py:132
  175.8 4.1 %all-to-all-done.2 = bf16[8,400,128]{2,1,0:T(8,128)(2,1)} async-done(((bf16[8,400,128]{2,1,0:T(8,128)(2,1)}), bf16[8,400,128]{2,1,0:T(8,128)(2,1)}, u32[]{:S(2)}, u32[]{:S(2)}) %all-to-all-start.2) | async-done | bytes 819232 | tf_op jit(solution)/shard_map/all_to_all | solution.py:162
  180.0 6.7 %all-to-all-start.1 = ((bf16[8,384,128]{2,1,0:T(8,128)(2,1)}), bf16[8,384,128]{2,1,0:T(8,128)(2,1)S(1)}, u32[]{:S(2)}, u32[]{:S(2)}) async-start(bf16[8,384,128]{2,1,0:T(8,128)(2,1)} %bitcast.21), calls=%async_computation.1 | async-start | bytes 1572864 | tf_op jit(solution)/shard_map/all_to_all | solution.py:135
  188.4 10.4 %all-to-all-done.1 = bf16[8,384,128]{2,1,0:T(8,128)(2,1)S(1)} async-done(((bf16[8,384,128]{2,1,0:T(8,128)(2,1)}), bf16[8,384,128]{2,1,0:T(8,128)(2,1)S(1)}, u32[]{:S(2)}, u32[]{:S(2)}) %all-to-all-start.1) | async-done | bytes 786464 | tf_op jit(solution)/shard_map/all_to_all | solution.py:135
  199.5 6.0 %all-to-all-start.3 = ((f32[8,16,360]{2,1,0:T(8,128)}), f32[8,16,360]{2,1,0:T(8,128)S(1)}, u32[]{:S(2)}, u32[]{:S(2)}) async-start(f32[8,16,360]{2,1,0:T(8,128)} %broadcast_in_dim.34), calls=%async_computation.3 | async-start | bytes 393216 | tf_op jit(solution)/shard_map/all_to_all | solution.py:26
  206.6 10.4 %all-to-all-done.3 = f32[8,16,360]{2,1,0:T(8,128)S(1)} async-done(((f32[8,16,360]{2,1,0:T(8,128)}), f32[8,16,360]{2,1,0:T(8,128)S(1)}, u32[]{:S(2)}, u32[]{:S(2)}) %all-to-all-start.3) | async-done | bytes 184352 | tf_op jit(solution)/shard_map/all_to_all | solution.py:26
  217.6 6.1 %all-to-all-start.4 = ((f32[8,16,360]{2,1,0:T(8,128)}), f32[8,16,360]{2,1,0:T(8,128)S(1)}, u32[]{:S(2)}, u32[]{:S(2)}) async-start(f32[8,16,360]{2,1,0:T(8,128)} %broadcast_in_dim.35), calls=%async_computation.4 | async-start | bytes 393216 | tf_op jit(solution)/shard_map/all_to_all | solution.py:26
  225.5 8.0 %all-to-all-done.4 = f32[8,16,360]{2,1,0:T(8,128)S(1)} async-done(((f32[8,16,360]{2,1,0:T(8,128)}), f32[8,16,360]{2,1,0:T(8,128)S(1)}, u32[]{:S(2)}, u32[]{:S(2)}) %all-to-all-start.4) | async-done | bytes 184352 | tf_op jit(solution)/shard_map/all_to_all | solution.py:26
  (129 shorter events, 32.8 us)
Async XLA Ops:
  7.2 179.5 %copy-start = (bf16[16,2880]{1,0:T(8,128)(2,1)S(1)}, bf16[16,2880]{1,0:T(8,128)(2,1)}, u32[]{:S(2)}) copy-start(bf16[16,2880]{1,0:T(8,128)(2,1)} %param.18) | copy-start | bytes 276484
  7.2 69.9 %all-gather.7.cloned.1.call-start = ((), (), s32[]{:S(2)}) async-start(), calls=%async_computation.5 | async-start | bytes 1769472 | tf_op jit(solution)/shard_map/all_gather | solution.py:82
  8.0 28.4 %copy-start.23 = (s32[128]{0:T(128)S(1)}, s32[128]{0:T(128)}, u32[]{:S(2)}) copy-start(s32[128]{0:T(128)} %param.19) | copy-start | bytes 1540
  8.0 30.3 %copy-start.1 = (bf16[128,2880]{0,1:T(8,128)(2,1)S(1)}, bf16[128,2880]{0,1:T(8,128)(2,1)}, u32[]{:S(2)}) copy-start(bf16[128,2880]{0,1:T(8,128)(2,1)} %param.11) | copy-start | bytes 2211844
  9.1 29.6 %copy-start.13 = (f32[2880]{0:T(1024)S(1)}, f32[2880]{0:T(1024)}, u32[]{:S(2)}) copy-start(f32[2880]{0:T(1024)} %param.12) | copy-start | bytes 34564
  9.1 29.6 %copy-start.14 = (f32[2880]{0:T(1024)S(1)}, f32[2880]{0:T(1024)}, u32[]{:S(2)}) copy-start(f32[2880]{0:T(1024)} %param.17) | copy-start | bytes 34564
  35.7 83.2 %all-gather.9.cloned.1.call-start = ((), (), s32[]{:S(2)}) async-start(), calls=%async_computation.6 | async-start | bytes 1769472 | tf_op jit(solution)/shard_map/all_gather | solution.py:81
  36.4 94.1 %collective-permute-start.1 = (s32[128]{0:T(128)S(1)}, s32[128]{0:T(128)S(1)}, u32[]{:S(2)}, u32[]{:S(2)}) collective-permute-start(s32[128]{0:T(128)S(1)} %copy-done.23), channel_id=1, source_target_pairs={{0,8},{8,16},{16,24},{24,32},{32,40},{40,48},{48,56},{56,64},{64,7... | collective-permute-start | bytes 1544 | tf_op jit(solution)/shard_map/ppermute | solution.py:20
  77.1 8.0 %copy-start.9 = (bf16[64,48,128]{2,1,0:T(8,128)(2,1)}, bf16[64,48,128]{2,1,0:T(8,128)(2,1)S(1)}, u32[]{:S(2)}) copy-start(bf16[64,48,128]{2,1,0:T(8,128)(2,1)S(1)} %all-gather.2) | copy-start | bytes 2359300
  77.1 55.5 %collective-permute-start.3 = (bf16[3072,256]{1,0:T(8,128)(2,1)}, bf16[3072,256]{1,0:T(8,128)(2,1)}, u32[]{:S(2)}, u32[]{:S(2)}) collective-permute-start(bf16[3072,256]{1,0:T(8,128)(2,1)} %bitcast.148), channel_id=1, source_target_pairs={{0,8},{8,0},{1,9},{9,1},{2,10},{10,2},{3,11},{11,3},{4,12},{12,4},... | collective-permute-start | bytes 4718600 | tf_op jit(solution)/shard_map/ppermute | solution.py:89
  79.7 66.2 %copy-start.15 = (bf16[128,128]{0,1:T(8,128)(2,1)}, bf16[128,128]{0,1:T(8,128)(2,1)S(1)}, u32[]{:S(2)}) copy-start(bf16[128,128]{0,1:T(8,128)(2,1)S(1)} %fusion.23) | copy-start | bytes 98308
  79.8 57.0 %collective-permute-start = (bf16[128,128]{0,1:T(8,128)(2,1)S(1)}, bf16[128,128]{0,1:T(8,128)(2,1)S(1)}, u32[]{:S(2)}, u32[]{:S(2)}) collective-permute-start(bf16[128,128]{0,1:T(8,128)(2,1)S(1)} %fusion.23), channel_id=1, source_target_pairs={{0,8},{8,16},{16,24},{24,32},{32,40},{40,48},{48,56},{56,64},{64,7... | collective-permute-start | bytes 98312 | tf_op jit(solution)/shard_map/ppermute | solution.py:20
  118.8 15.8 %collective-permute-start.2 = (bf16[3072,256]{1,0:T(8,128)(2,1)}, bf16[3072,256]{1,0:T(8,128)(2,1)}, u32[]{:S(2)}, u32[]{:S(2)}) collective-permute-start(bf16[3072,256]{1,0:T(8,128)(2,1)} %bitcast.151), channel_id=1, source_target_pairs={{0,8},{8,0},{1,9},{9,1},{2,10},{10,2},{3,11},{11,3},{4,12},{12,4},... | collective-permute-start | bytes 4718600 | tf_op jit(solution)/shard_map/ppermute | solution.py:88
  136.7 16.6 %copy-start.11 = (bf16[512,128]{1,0:T(8,128)(2,1)}, bf16[512,128]{1,0:T(8,128)(2,1)S(1)}, u32[]{:S(2)}) copy-start(bf16[512,128]{1,0:T(8,128)(2,1)S(1)} %pad_maximum_fusion.1) | copy-start | bytes 393220
  136.7 9.2 %copy-start.17 = (bf16[128,128]{0,1:T(8,128)(2,1)}, bf16[128,128]{0,1:T(8,128)(2,1)S(1)}, u32[]{:S(2)}) copy-start(bf16[128,128]{0,1:T(8,128)(2,1)S(1)} %collective-permute-done) | copy-start | bytes 98308
  138.8 7.2 %copy-start.25 = (f32[8,128]{1,0:T(8,128)}, f32[8,128]{1,0:T(8,128)S(1)}, u32[]{:S(2)}) copy-start(f32[8,128]{1,0:T(8,128)S(1)} %get-tuple-element.19) | copy-start | bytes 12292
  156.4 3.1 %collective-permute-start.4 = (bf16[128,128]{1,0:T(8,128)(2,1)S(1)}, bf16[128,128]{1,0:T(8,128)(2,1)S(1)}, u32[]{:S(2)}, u32[]{:S(2)}) collective-permute-start(bf16[128,128]{1,0:T(8,128)(2,1)S(1)} %fusion.50), channel_id=1, source_target_pairs={{8,0},{16,8},{24,16},{32,24},{40,32},{48,40},{56,48},{64,56},{72,6... | collective-permute-start | bytes 98312 | tf_op jit(solution)/shard_map/ppermute | solution.py:20
  162.3 6.9 %copy-start.12 = (bf16[512,128]{1,0:T(8,128)(2,1)S(1)}, bf16[512,128]{1,0:T(8,128)(2,1)}, u32[]{:S(2)}) copy-start(bf16[512,128]{1,0:T(8,128)(2,1)} %copy-done.11) | copy-start | bytes 393220
  163.3 16.6 %all-to-all-start.2 = ((bf16[8,400,128]{2,1,0:T(8,128)(2,1)}), bf16[8,400,128]{2,1,0:T(8,128)(2,1)}, u32[]{:S(2)}, u32[]{:S(2)}) async-start(bf16[8,400,128]{2,1,0:T(8,128)(2,1)} %pad_maximum_fusion), calls=%async_computation.2 | async-start | bytes 1638400 | tf_op jit(solution)/shard_map/all_to_all | solution.py:162
  174.8 11.8 %copy-start.22 = (s32[128]{0:T(128)S(1)}, s32[128]{0:T(128)}, u32[]{:S(2)}) copy-start(s32[128]{0:T(128)} %param.20) | copy-start | bytes 1540
  179.9 8.2 %copy-start.24 = (f32[128]{0:T(128)S(1)}, f32[128]{0:T(128)}, u32[]{:S(2)}) copy-start(f32[128]{0:T(128)} %get-tuple-element.8) | copy-start | bytes 1540
  180.0 18.9 %all-to-all-start.1 = ((bf16[8,384,128]{2,1,0:T(8,128)(2,1)}), bf16[8,384,128]{2,1,0:T(8,128)(2,1)S(1)}, u32[]{:S(2)}, u32[]{:S(2)}) async-start(bf16[8,384,128]{2,1,0:T(8,128)(2,1)} %bitcast.21), calls=%async_computation.1 | async-start | bytes 1572864 | tf_op jit(solution)/shard_map/all_to_all | solution.py:135
  199.5 17.4 %all-to-all-start.3 = ((f32[8,16,360]{2,1,0:T(8,128)}), f32[8,16,360]{2,1,0:T(8,128)S(1)}, u32[]{:S(2)}, u32[]{:S(2)}) async-start(f32[8,16,360]{2,1,0:T(8,128)} %broadcast_in_dim.34), calls=%async_computation.3 | async-start | bytes 393216 | tf_op jit(solution)/shard_map/all_to_all | solution.py:26
  217.6 15.8 %all-to-all-start.4 = ((f32[8,16,360]{2,1,0:T(8,128)}), f32[8,16,360]{2,1,0:T(8,128)S(1)}, u32[]{:S(2)}, u32[]{:S(2)}) async-start(f32[8,16,360]{2,1,0:T(8,128)} %broadcast_in_dim.35), calls=%async_computation.4 | async-start | bytes 393216 | tf_op jit(solution)/shard_map/all_to_all | solution.py:26
  (14 other events, 46.9 us)
Sparse Core Ops, SparseCore 0:
  35.8 39.7 all-gather.6
  77.7 41.1 all-gather.8
where the time goes:
time: 242 us; the launch traced here: 241 us
  waiting for transfers between devices  68.4 us (28%)
  blocking collectives  61.7 us (25%)
  matrix products  35.3 us (15%)
  starting transfers between devices  34.4 us (14%)
  local copies, waits for them, and re-layouts  17 us (7%)
  between operations  14.7 us (6%)
  other arithmetic  9.35 us (4%)
    all_gather x1, waiting for transfers between devices, shards(): lax.all_gather(near[:, 0], 'y', axis=0, tiled=True).reshape(-1, half)  33.8 us
    all_to_all x1, blocking collectives, shards(): near = lax.all_to_all(sent, ('zh', 'core'), 0, 0)  25.7 us
    all_gather x1, blocking collectives, shards(): kv_all = lax.all_gather(kv_near, ('y', 'core'), axis=0, tiled=False)  22.2 us
    all_to_all x2, waiting for transfers between devices, gathered(): return lax.all_to_all(spread, axes, 0, 0)  18.3 us
    all_gather x1, blocking collectives, shards(): kv_near = lax.all_gather(w_kv, ('zh',), axis=0, tiled=False)  13.8 us
    dot_general x13, matrix products, dot(): lax.dot_general(left, right, (dims, ((), ())), preferred_element_type=F32...  12.8 us
    all_to_all x2, starting transfers between devices, gathered(): return lax.all_to_all(spread, axes, 0, 0)  12.1 us
    all_to_all x1, waiting for transfers between devices, shards(): attn = lax.all_to_all(for_heads(term.astype(BF16)), HEAD, 0, 0)  10.4 us
  transfers between devices with their start and end apart: 11, of which 6 were waited for; matrix products, arithmetic and copies ran while one was open for 13% of the time, Pallas kernels for 0%

commit v1 on v0

--- a/solution.py
+++ b/solution.py
@@ -78,7 +78,13 @@
     both = both.reshape(2, PAD, 2, half).transpose(2, 0, 1, 3)
     sent = jnp.broadcast_to(both[None], (4,) + both.shape).reshape((8,) + both.shape[1:])
     near = lax.all_to_all(sent, ("zh", "core"), 0, 0)
-    q_own = lax.all_gather(near[:, 0], "y", axis=0, tiled=True).reshape(-1, half)
+    serve_clusters_by_axis = lambda local_x, device_axis: jnp.concatenate(
+        lax.all_to_all(
+            jnp.stack([local_x] * lax.axis_size(device_axis), axis=0), device_axis, 0, 0
+        ),
+        axis=0,
+    )
+    q_own = serve_clusters_by_axis(near[:, 0], device_axis="y").reshape(-1, half)
     o_own = lax.all_gather(near[:, 1], "y", axis=0, tiled=True).reshape(-1, half)
     w_kv = padded(jnp.concatenate([w_key, w_value], axis=1))
     kv_near = lax.all_gather(w_kv, ("zh",), axis=0, tiled=False)

time: 242 us -> 247 us (1.021)
  waiting for transfers between devices: 68.4 us -> 37.3 us
  blocking collectives: 61.7 us -> 83.6 us
  local copies, waits for them, and re-layouts: 17 us -> 25.5 us
  matrix products: 35.3 us -> 39.8 us
    all_gather x1 -> x0, waiting for transfers between devices: 33.8 us -> none  [shards(): lax.all_gather(near[:, 0], 'y', axis=0, tiled=True).reshape(-1, half)]
    all_gather x1, blocking collectives: 22.2 us -> 44.2 us  [shards(): kv_all = lax.all_gather(kv_near, ('y', 'core'), axis=0, tiled=False)]
    all_to_all x0 -> x1, starting transfers between devices: none -> 7.23 us  [shards(): lax.all_to_all(jnp.stack([local_x] * lax.axis_size(device_axis), axis=0),...]
    all_to_all x2, starting transfers between devices: 12.1 us -> 7.89 us  [gathered(): return lax.all_to_all(spread, axes, 0, 0)]
    reshape x4, local copies, waits for them, and re-layouts: 3.01 us -> 6.92 us  [blocked(): parts = rows.reshape(4, 8, 2, -1, width).transpose(1, 0, 2, 3, 4)]
    unnamed x56 -> x46, local copies, waits for them, and re-layouts: 4.24 us -> 5.44 us
  transfers between devices with their start and end apart: 11 -> 11, of which waited for: 6 -> 4; matrix products, arithmetic and copies ran while one was open for 13% -> 20% of each run, Pallas kernels for 0% -> 0%
where the time goes in v1:
time: 247 us; the launch traced here: 246 us
  blocking collectives  83.6 us (34%)
  matrix products  39.8 us (16%)
  waiting for transfers between devices  37.3 us (15%)
  starting transfers between devices  35.1 us (14%)
  local copies, waits for them, and re-layouts  25.5 us (10%)
  between operations  14.6 us (6%)
  other arithmetic  10.1 us (4%)
    all_gather x1, blocking collectives, shards(): kv_all = lax.all_gather(kv_near, ('y', 'core'), axis=0, tiled=False)  44.2 us
    all_to_all x1, blocking collectives, shards(): near = lax.all_to_all(sent, ('zh', 'core'), 0, 0)  25.7 us
    all_to_all x2, waiting for transfers between devices, gathered(): return lax.all_to_all(spread, axes, 0, 0)  19.7 us
    dot_general x13, matrix products, dot(): lax.dot_general(left, right, (dims, ((), ())), preferred_element_type=F32...  14.7 us
    all_gather x1, blocking collectives, shards(): kv_near = lax.all_gather(w_kv, ('zh',), axis=0, tiled=False)  13.7 us
    all_to_all x1, waiting for transfers between devices, shards(): attn = lax.all_to_all(for_heads(term.astype(BF16)), HEAD, 0, 0)  10.7 us
    all_to_all x2, starting transfers between devices, gathered(): return lax.all_to_all(spread, axes, 0, 0)  7.89 us
    dot_general x1, matrix products, shards(): jnp.einsum('hqk,dk->hdq', grad_scores, keys, preferred_element_type=F32)  7.89 us
  transfers between devices with their start and end apart: 11, of which 4 were waited for; matrix products, arithmetic and copies ran while one was open for 20% of the time, Pallas kernels for 0%

profile of v1, /device:TPU:2, one launch (start us, length us, event | category | flops | bytes accessed | tf_op | source)
XLA Modules:
  0.0 246.0 jit_solution(12845057809641088719)
XLA Ops:
  9.1 25.7 %all_to_all.30 = bf16[8,2,48,256]{3,2,1,0:T(8,128)(2,1)S(1)} all-to-all(bf16[8,2,48,256]{3,2,1,0:T(8,128)(2,1)S(1)} %bitcast.167), channel_id=1, replica_groups=mesh['zh'=4,'y'=8,'core'=2,'x'=4,'zl'=2] {'zh','core'}, dimensions={0} | all-to-all | bytes 786432 | tf_op jit(solution)/shard_map/all_to_all | solution.py:80
  36.7 7.2 %all-to-all-start.1 = ((bf16[8,8,48,256]{3,2,1,0:T(8,128)(2,1)}), bf16[8,8,48,256]{3,2,1,0:T(8,128)(2,1)S(1)}, u32[]{:S(2)}, u32[]{:S(2)}) async-start(bf16[8,8,48,256]{3,2,1,0:T(8,128)(2,1)} %stack.22), calls=%async_computation.1 | async-start | bytes 3145728 | tf_op jit(solution)/shard_map/all_to_all | solution.py:82
  49.1 13.7 %all-gather.1 = bf16[192,128]{1,0:T(8,128)(2,1)S(1)} all-gather(bf16[48,128]{1,0:T(8,128)(2,1)S(1)} %fusion.63), channel_id=3, replica_groups=mesh['zh'=4,'y'=8,'core'=2,'x'=4,'zl'=2] {'zh'}, dimensions={0}, use_global_device_ids=true | all-gather | bytes 61440 | tf_op jit(solution)/shard_map/all_gather | solution.py:90
  62.8 44.2 %all-gather.2 = bf16[64,48,128]{2,1,0:T(8,128)(2,1)} all-gather(bf16[4,48,128]{2,1,0:T(8,128)(2,1)S(1)} %bitcast.176), channel_id=4, replica_groups=mesh['zh'=4,'y'=8,'core'=2,'x'=4,'zl'=2] {'y','core'}, dimensions={0}, use_global_device_ids=true | all-gather | bytes 835584 | tf_op jit(solution)/shard_map/all_gather | solution.py:91
  107.0 2.2 collective-permute-start.2
  115.0 2.5 %fusion.10 = (f32[128]{0:T(128)S(1)}, f32[2880,128]{1,0:T(8,128)}) fusion(bf16[128,2880]{0,1:T(8,128)(2,1)S(1)} %copy-done.1, f32[2880]{0:T(1024)S(1)} %mul.187, f32[128]{0:T(128)S(1)} %add_rsqrt_fusion, f32[2880]{0:T(1024)S(1)} %copy-done.13), kind=kLoop, calls=%fused_computation.17 | loop fusion | flops 1843072 | bytes 2235904 | tf_op jit(solution)/shard_map/reduce_sum | solution.py:173
  117.6 2.2 collective-permute-start.3
  126.4 2.5 %reshape.219 = f32[4,8,2,45,128]{4,3,2,1,0:T(8,128)} reshape(f32[2880,128]{1,0:T(8,128)} %get-tuple-element.9) | data formatting | bytes 2949120 | tf_op jit(solution)/shard_map/reshape | solution.py:35
  128.9 2.7 %copy.63 = f32[8,4,2,45,128]{4,3,2,1,0:T(8,128)} copy(f32[8,4,2,45,128]{4,3,2,0,1:T(8,128)} %bitcast.156) | data formatting | bytes 2949120
  131.6 2.7 %pad.31.clone = f32[8,4,2,48,128]{4,3,2,1,0:T(8,128)} pad(f32[8,4,2,45,128]{4,3,2,1,0:T(8,128)} %copy.63, f32[]{:T(128)} %constant.42.clone.1), padding=0_0x0_0x0_0x0_3x0_0 | pad | bytes 3047428 | tf_op jit(solution)/shard_map/jit(_pad)/pad | solution.py:36
  142.4 3.1 %fusion.106 = (f32[8,128]{1,0:T(8,128)}, f32[8,128,256]{2,1,0:T(8,128)}) fusion(bf16[8,64,128]{2,1,0:T(8,128)(2,1)} %bitcast.177, pred[128,256]{1,0:T(8,128)(4,1)} %fusion.43, bf16[128,128]{0,1:T(8,128)(2,1)S(1)} %fusion.23, bf16[128,128]{0,1:T(8,128)(2,1)S(1)} %collective-permute-done), kind=kOutput, calls=%fused_computation.137 | convolution fusion | flops 34668800 | bytes 1282048 | tf_op jit(solution)/shard_map/sub | solution.py:135
  145.4 7.1 %convolution_bitcast_fusion.2 = f32[64,256]{1,0:T(8,128)S(1)} fusion(bf16[8,64,128]{2,1,0:T(8,128)(2,1)} %bitcast.178, f32[8,128,256]{2,1,0:T(8,128)S(1)} %fusion.65, f32[8,128,256]{2,1,0:T(8,128)} %get-tuple-element.20, f32[8,128]{1,0:T(8,128)} %get-tuple-element.19), kind=kOutput, calls=%fused_computation.41 | convolution fusion | flops 35390720 | bytes 2297856 | tf_op jit(solution)/shard_map/hqk,hdq->dk/dot_general | solution.py:157
  152.6 3.6 %convolution_bitcast_fusion.1 = f32[64,256]{1,0:T(8,128)} fusion(bf16[8,64,128]{2,1,0:T(8,128)(2,1)} %bitcast.171, f32[8,128]{1,0:T(8,128)} %get-tuple-element.19, bf16[8,64,128]{2,1,0:T(8,128)(2,1)} %bitcast.179, pred[128,256]{1,0:T(8,128)(4,1)} %fusion.43, bf16[128,128]{0,1:T(8,128)(2,1)} %copy-done.15, bf16[128,128]{0,1:T(8,128)(2,1)} %copy-done.17), kind=kOutput, calls=%fused_computation.40 | convolution fusion | flops 68486400 | bytes 430080 | tf_op jit(solution)/shard_map/hqk,hdq->dk/dot_general | solution.py:151
  159.0 7.9 %fusion.21 = bf16[8,64,128]{2,1,0:T(8,128)(2,1)} fusion(f32[8,128,256]{2,1,0:T(8,128)S(1)} %fusion.65, bf16[128,128]{0,1:T(8,128)(2,1)} %copy-done.15, bf16[128,128]{0,1:T(8,128)(2,1)} %copy-done.17, f32[8,128,256]{2,1,0:T(8,128)} %get-tuple-element.20, f32[8,128]{1,0:T(8,128)} %get-tuple-element.19), kind=kOutput, calls=%fused_computation.33 | convolution fusion | flops 35521792 | bytes 2297856 | tf_op jit(solution)/shard_map/hqk,dk->hdq/dot_general | solution.py:155
  170.0 2.3 fusion.7
  173.4 4.7 %all-to-all-start.3 = ((bf16[8,400,128]{2,1,0:T(8,128)(2,1)}), bf16[8,400,128]{2,1,0:T(8,128)(2,1)S(1)}, u32[]{:S(2)}, u32[]{:S(2)}) async-start(bf16[8,400,128]{2,1,0:T(8,128)(2,1)} %pad_maximum_fusion), calls=%async_computation.3 | async-start | bytes 1638400 | tf_op jit(solution)/shard_map/all_to_all | solution.py:168
  178.1 3.1 %fusion.20 = bf16[8,64,128]{2,1,0:T(8,128)(2,1)S(1)} fusion(bf16[128,128]{0,1:T(8,128)(2,1)S(1)} %copy-done.16, bf16[128,128]{0,1:T(8,128)(2,1)} %copy-done.17, f32[8,128]{1,0:T(8,128)} %get-tuple-element.19, bf16[8,64,128]{2,1,0:T(8,128)(2,1)S(1)} %bitcast.180, pred[128,256]{1,0:T(8,128)(4,1)} %fusion.43), kind=kOutput, calls=%fused_computation.32 | convolution fusion | flops 68617472 | bytes 430080 | tf_op jit(solution)/shard_map/hqk,dk->hdq/dot_general | solution.py:138
  184.7 6.2 %all-to-all-done.3 = bf16[8,400,128]{2,1,0:T(8,128)(2,1)S(1)} async-done(((bf16[8,400,128]{2,1,0:T(8,128)(2,1)}), bf16[8,400,128]{2,1,0:T(8,128)(2,1)S(1)}, u32[]{:S(2)}, u32[]{:S(2)}) %all-to-all-start.3) | async-done | bytes 819232 | tf_op jit(solution)/shard_map/all_to_all | solution.py:168
  190.9 5.2 %all-to-all-start.2 = ((bf16[8,384,128]{2,1,0:T(8,128)(2,1)}), bf16[8,384,128]{2,1,0:T(8,128)(2,1)S(1)}, u32[]{:S(2)}, u32[]{:S(2)}) async-start(bf16[8,384,128]{2,1,0:T(8,128)(2,1)} %bitcast.22), calls=%async_computation.2 | async-start | bytes 1572864 | tf_op jit(solution)/shard_map/all_to_all | solution.py:141
  196.7 10.7 %all-to-all-done.2 = bf16[8,384,128]{2,1,0:T(8,128)(2,1)S(1)} async-done(((bf16[8,384,128]{2,1,0:T(8,128)(2,1)}), bf16[8,384,128]{2,1,0:T(8,128)(2,1)S(1)}, u32[]{:S(2)}, u32[]{:S(2)}) %all-to-all-start.2) | async-done | bytes 786464 | tf_op jit(solution)/shard_map/all_to_all | solution.py:141
  208.1 3.4 %all-to-all-start.4 = ((f32[8,16,360]{2,1,0:T(8,128)}), f32[8,16,360]{2,1,0:T(8,128)S(1)}, u32[]{:S(2)}, u32[]{:S(2)}) async-start(f32[8,16,360]{2,1,0:T(8,128)} %broadcast_in_dim.34), calls=%async_computation.4 | async-start | bytes 393216 | tf_op jit(solution)/shard_map/all_to_all | solution.py:26
  211.8 11.0 %all-to-all-done.4 = f32[8,16,360]{2,1,0:T(8,128)S(1)} async-done(((f32[8,16,360]{2,1,0:T(8,128)}), f32[8,16,360]{2,1,0:T(8,128)S(1)}, u32[]{:S(2)}, u32[]{:S(2)}) %all-to-all-start.4) | async-done | bytes 184352 | tf_op jit(solution)/shard_map/all_to_all | solution.py:26
  223.4 4.5 %all-to-all-start.5 = ((f32[8,16,360]{2,1,0:T(8,128)}), f32[8,16,360]{2,1,0:T(8,128)S(1)}, u32[]{:S(2)}, u32[]{:S(2)}) async-start(f32[8,16,360]{2,1,0:T(8,128)} %broadcast_in_dim.35), calls=%async_computation.5 | async-start | bytes 393216 | tf_op jit(solution)/shard_map/all_to_all | solution.py:26
  229.7 8.8 %all-to-all-done.5 = f32[8,16,360]{2,1,0:T(8,128)S(1)} async-done(((f32[8,16,360]{2,1,0:T(8,128)}), f32[8,16,360]{2,1,0:T(8,128)S(1)}, u32[]{:S(2)}, u32[]{:S(2)}) %all-to-all-start.5) | async-done | bytes 184352 | tf_op jit(solution)/shard_map/all_to_all | solution.py:26
  (119 shorter events, 44.4 us)
Async XLA Ops:
  7.2 188.9 %copy-start = (bf16[16,2880]{1,0:T(8,128)(2,1)S(1)}, bf16[16,2880]{1,0:T(8,128)(2,1)}, u32[]{:S(2)}) copy-start(bf16[16,2880]{1,0:T(8,128)(2,1)} %param.18) | copy-start | bytes 276484
  36.7 8.0 %copy-start.1 = (bf16[128,2880]{0,1:T(8,128)(2,1)S(1)}, bf16[128,2880]{0,1:T(8,128)(2,1)}, u32[]{:S(2)}) copy-start(bf16[128,2880]{0,1:T(8,128)(2,1)} %param.11) | copy-start | bytes 2211844
  36.7 8.4 %copy-start.13 = (f32[2880]{0:T(1024)S(1)}, f32[2880]{0:T(1024)}, u32[]{:S(2)}) copy-start(f32[2880]{0:T(1024)} %param.12) | copy-start | bytes 34564
  36.7 8.4 %copy-start.14 = (f32[2880]{0:T(1024)S(1)}, f32[2880]{0:T(1024)}, u32[]{:S(2)}) copy-start(f32[2880]{0:T(1024)} %param.17) | copy-start | bytes 34564
  36.7 70.3 %all-to-all-start.1 = ((bf16[8,8,48,256]{3,2,1,0:T(8,128)(2,1)}), bf16[8,8,48,256]{3,2,1,0:T(8,128)(2,1)S(1)}, u32[]{:S(2)}, u32[]{:S(2)}) async-start(bf16[8,8,48,256]{3,2,1,0:T(8,128)(2,1)} %stack.22), calls=%async_computation.1 | async-start | bytes 3145728 | tf_op jit(solution)/shard_map/all_to_all | solution.py:82
  43.9 73.6 %all-gather.5.cloned.1.call-start = ((), (), s32[]{:S(2)}) async-start(), calls=%async_computation.6 | async-start | bytes 1769472 | tf_op jit(solution)/shard_map/all_gather | solution.py:88
  49.0 68.6 %copy-start.8 = (bf16[4,8,2,45,128]{4,3,2,0,1:T(8,128)(2,1)}, bf16[4,8,2,45,128]{4,3,2,0,1:T(8,128)(2,1)S(1)}, u32[]{:S(2)}) copy-start(bf16[4,8,2,45,128]{4,3,2,0,1:T(8,128)(2,1)S(1)} %copy.69) | copy-start | bytes 2211844
  49.0 63.9 %copy-start.21 = (s32[128]{0:T(128)S(1)}, s32[128]{0:T(128)}, u32[]{:S(2)}) copy-start(s32[128]{0:T(128)} %param.19) | copy-start | bytes 1540
  107.0 29.6 %collective-permute-start.2 = (bf16[3072,256]{1,0:T(8,128)(2,1)S(1)}, bf16[3072,256]{1,0:T(8,128)(2,1)}, u32[]{:S(2)}, u32[]{:S(2)}) collective-permute-start(bf16[3072,256]{1,0:T(8,128)(2,1)S(1)} %bitcast.146), channel_id=1, source_target_pairs={{0,8},{8,0},{1,9},{9,1},{2,10},{10,2},{3,11},{11,3},{4,12},{12,4},... | collective-permute-start | bytes 4718600 | tf_op jit(solution)/shard_map/ppermute | solution.py:94
  110.8 31.6 %copy-start.15 = (bf16[128,128]{0,1:T(8,128)(2,1)}, bf16[128,128]{0,1:T(8,128)(2,1)S(1)}, u32[]{:S(2)}) copy-start(bf16[128,128]{0,1:T(8,128)(2,1)S(1)} %fusion.23) | copy-start | bytes 98308
  110.8 30.6 %collective-permute-start = (bf16[128,128]{0,1:T(8,128)(2,1)S(1)}, bf16[128,128]{0,1:T(8,128)(2,1)S(1)}, u32[]{:S(2)}, u32[]{:S(2)}) collective-permute-start(bf16[128,128]{0,1:T(8,128)(2,1)S(1)} %fusion.23), channel_id=1, source_target_pairs={{0,8},{8,16},{16,24},{24,32},{32,40},{40,48},{48,56},{56,64},{64,7... | collective-permute-start | bytes 98312 | tf_op jit(solution)/shard_map/ppermute | solution.py:20
  112.9 21.5 %collective-permute-start.1 = (s32[128]{0:T(128)S(1)}, s32[128]{0:T(128)S(1)}, u32[]{:S(2)}, u32[]{:S(2)}) collective-permute-start(s32[128]{0:T(128)S(1)} %copy-done.21), channel_id=1, source_target_pairs={{0,8},{8,16},{16,24},{24,32},{32,40},{40,48},{48,56},{56,64},{64,7... | collective-permute-start | bytes 1544 | tf_op jit(solution)/shard_map/ppermute | solution.py:20
  117.6 3.5 %copy-start.9 = (bf16[64,48,128]{2,1,0:T(8,128)(2,1)S(1)}, bf16[64,48,128]{2,1,0:T(8,128)(2,1)}, u32[]{:S(2)}) copy-start(bf16[64,48,128]{2,1,0:T(8,128)(2,1)} %all-gather.2) | copy-start | bytes 2359300
  117.6 21.7 %collective-permute-start.3 = (bf16[3072,256]{1,0:T(8,128)(2,1)}, bf16[3072,256]{1,0:T(8,128)(2,1)}, u32[]{:S(2)}, u32[]{:S(2)}) collective-permute-start(bf16[3072,256]{1,0:T(8,128)(2,1)} %bitcast.153), channel_id=1, source_target_pairs={{0,8},{8,0},{1,9},{9,1},{2,10},{10,2},{3,11},{11,3},{4,12},{12,4},... | collective-permute-start | bytes 4718600 | tf_op jit(solution)/shard_map/ppermute | solution.py:95
  141.4 4.1 %copy-start.17 = (bf16[128,128]{0,1:T(8,128)(2,1)}, bf16[128,128]{0,1:T(8,128)(2,1)S(1)}, u32[]{:S(2)}) copy-start(bf16[128,128]{0,1:T(8,128)(2,1)S(1)} %collective-permute-done) | copy-start | bytes 98308
  157.5 10.8 %collective-permute-start.4 = (bf16[128,128]{1,0:T(8,128)(2,1)}, bf16[128,128]{1,0:T(8,128)(2,1)}, u32[]{:S(2)}, u32[]{:S(2)}) collective-permute-start(bf16[128,128]{1,0:T(8,128)(2,1)} %fusion.50), channel_id=1, source_target_pairs={{8,0},{16,8},{24,16},{32,24},{40,32},{48,40},{56,48},{64,56},{72,6... | collective-permute-start | bytes 98312 | tf_op jit(solution)/shard_map/ppermute | solution.py:20
  172.4 5.6 %copy-start.12 = (bf16[512,128]{1,0:T(8,128)(2,1)S(1)}, bf16[512,128]{1,0:T(8,128)(2,1)}, u32[]{:S(2)}) copy-start(bf16[512,128]{1,0:T(8,128)(2,1)} %pad_maximum_fusion.1) | copy-start | bytes 393220
  172.4 5.6 %copy-start.16 = (bf16[128,128]{0,1:T(8,128)(2,1)S(1)}, bf16[128,128]{0,1:T(8,128)(2,1)}, u32[]{:S(2)}) copy-start(bf16[128,128]{0,1:T(8,128)(2,1)} %copy-done.15) | copy-start | bytes 98308
  173.4 17.5 %all-to-all-start.3 = ((bf16[8,400,128]{2,1,0:T(8,128)(2,1)}), bf16[8,400,128]{2,1,0:T(8,128)(2,1)S(1)}, u32[]{:S(2)}, u32[]{:S(2)}) async-start(bf16[8,400,128]{2,1,0:T(8,128)(2,1)} %pad_maximum_fusion), calls=%async_computation.3 | async-start | bytes 1638400 | tf_op jit(solution)/shard_map/all_to_all | solution.py:168
  183.7 12.4 %copy-start.6 = (bf16[128,2880]{0,1:T(8,128)(2,1)S(1)}, bf16[128,2880]{0,1:T(8,128)(2,1)}, u32[]{:S(2)}) copy-start(bf16[128,2880]{0,1:T(8,128)(2,1)} %param.21) | copy-start | bytes 2211844
  183.7 12.4 %copy-start.20 = (s32[128]{0:T(128)S(1)}, s32[128]{0:T(128)}, u32[]{:S(2)}) copy-start(s32[128]{0:T(128)} %param.20) | copy-start | bytes 1540
  190.9 16.5 %all-to-all-start.2 = ((bf16[8,384,128]{2,1,0:T(8,128)(2,1)}), bf16[8,384,128]{2,1,0:T(8,128)(2,1)S(1)}, u32[]{:S(2)}, u32[]{:S(2)}) async-start(bf16[8,384,128]{2,1,0:T(8,128)(2,1)} %bitcast.22), calls=%async_computation.2 | async-start | bytes 1572864 | tf_op jit(solution)/shard_map/all_to_all | solution.py:141
  208.1 14.7 %all-to-all-start.4 = ((f32[8,16,360]{2,1,0:T(8,128)}), f32[8,16,360]{2,1,0:T(8,128)S(1)}, u32[]{:S(2)}, u32[]{:S(2)}) async-start(f32[8,16,360]{2,1,0:T(8,128)} %broadcast_in_dim.34), calls=%async_computation.4 | async-start | bytes 393216 | tf_op jit(solution)/shard_map/all_to_all | solution.py:26
  223.4 15.1 %all-to-all-start.5 = ((f32[8,16,360]{2,1,0:T(8,128)}), f32[8,16,360]{2,1,0:T(8,128)S(1)}, u32[]{:S(2)}, u32[]{:S(2)}) async-start(f32[8,16,360]{2,1,0:T(8,128)} %broadcast_in_dim.35), calls=%async_computation.5 | async-start | bytes 393216 | tf_op jit(solution)/shard_map/all_to_all | solution.py:26
  (9 other events, 15.3 us)
Sparse Core Ops, SparseCore 0:
  46.9 55.2 all-gather.4
